TPU v7x, 128 devices: a whole 4x4x4 slice. The times are simulated.
128 devices in a mesh: dp: 4 (over z), latent: 32 (over x, y, core).
Axes of the slice: x: 4, y: 4, z: 4, core: 2. Of those that a mesh axis runs over, the one named last changes fastest.
Arguments:
- acts: bfloat16 [640, 8192], P(('dp', 'latent')), may hold values from -6 to 6
- chat_len: int32 [128], P(('dp', 'latent')), may hold values from 1 to 5, as said below
- group_of: int32 [640, 1], P(('dp', 'latent')), may hold values from 0 to 4; in each aligned block of 5 rows (0 to 4, 5 to 9, ...) no two rows name the same one
- w_enc: bfloat16 [2, 4096, 16384], P(None, None, 'latent'), may hold values from -0.0625 to 0.0625
- b_enc: float32 [16384], P('latent'), may hold values from -3 to 3
- w_dec: bfloat16 [16384, 8192], P('latent'), may hold values from -0.046875 to 0.046875
- b_dec: float32 [2, 4096], replicated, may hold values from -3 to 3
Outputs:
- grad_enc: bfloat16 [2, 4096, 16384], P(None, 'dp', 'latent')
- grad_dec: bfloat16 [16384, 8192], P('latent', 'dp')
- loss: float32 [], replicated
Inputs may be any that keep to these rules, and one draw needn't show every extreme that they name: `chat_len`: the last serving shard harvests all 5 rows. `group_of`: among the 5 row slots of each serving shard every value 0 to 4 appears exactly once.
All inputs are finite; a program needn't handle non-finite values.
Results may differ from a plain program's by a relative error of at most 0.02.
Values may be sent and summed in bfloat16 or wider, within the bound.
No kernel may reach another device: no remote copies, remote signals or barrier semaphores. Data moves between devices by JAX's collectives and lax.ppermute only.
A program may use at most 128 MiB of HBM per device.

v0:
```python
import jax
import jax.numpy as jnp
from jax import lax
from jax.sharding import PartitionSpec as P

sparsity_weight = 1.0
loss_scale = 8.0
norm_eps = 1e-06


def shards(acts, chat_len, group_of, w_enc, b_enc, w_dec, b_dec):
    groups = lax.axis_size("dp")
    slots = acts.shape[0]
    width = acts.shape[1]
    half = width // 2
    local_latents = w_enc.shape[2]
    capacity = slots // (groups + 1)
    slot_ids = jnp.arange(slots, dtype=jnp.int32)
    alive = (slot_ids < chat_len[0]).astype(jnp.float32)
    order = jnp.argsort(group_of[:, 0], stable=True)[: groups * capacity]
    own_count = jnp.sum(alive[order])
    outgoing = acts[order].reshape(groups, capacity, width)
    out_mask = alive[order].reshape(groups, capacity).astype(jnp.bfloat16)
    received, recv_mask = (
        lax.all_to_all(outgoing, "dp", split_axis=0, concat_axis=0, tiled=True),
        lax.all_to_all(out_mask, "dp", split_axis=0, concat_axis=0, tiled=True),
    )
    member_rows, member_mask = (
        lax.all_gather(received, "latent", axis=0, tiled=True),
        lax.all_gather(recv_mask, "latent", axis=0, tiled=True),
    )
    xg = member_rows.reshape(-1, width)
    maskg = member_mask.reshape(-1).astype(jnp.float32)
    total_rows = xg.shape[0]
    share_rows = total_rows // lax.axis_size("latent")
    first_row = lax.axis_index("latent") * share_rows
    wenc_flat = w_enc.reshape(width, local_latents)
    squares_dec = jnp.square(w_dec.astype(jnp.float32))
    norm_base = jnp.sqrt(jnp.sum(squares_dec[:, :half], axis=1) + norm_eps)
    norm_inst = jnp.sqrt(jnp.sum(squares_dec[:, half:], axis=1) + norm_eps)
    norm_sum = norm_base + norm_inst
    column_ids = jnp.arange(width, dtype=jnp.int32)
    bias_row = b_dec.reshape(width)
    pre = jnp.dot(xg, wenc_flat, preferred_element_type=jnp.float32) + b_enc[None, :]
    act = jnp.maximum(pre, 0.0)
    feats = act * act
    feats16 = feats.astype(jnp.bfloat16)
    partial_value = jnp.dot(feats16, w_dec, preferred_element_type=jnp.float32)
    recon = lax.psum(partial_value.astype(jnp.bfloat16), "latent").astype(jnp.float32)
    err = (recon + bias_row[None, :] - xg.astype(jnp.float32)) * maskg[:, None]
    err16 = err.astype(jnp.bfloat16)
    err_share = lax.dynamic_slice_in_dim(err, first_row, share_rows, 0)
    square_sum = jnp.sum(err_share * err_share)
    feat_sum = jnp.sum(feats * maskg[:, None], axis=0)
    local_loss = square_sum + sparsity_weight * jnp.sum(feat_sum * norm_sum)
    dfeat = 2.0 * lax.dot_general(
        err16, w_dec, (((1,), (1,)), ((), ())), preferred_element_type=jnp.float32
    )
    dfeat = dfeat + sparsity_weight * maskg[:, None] * norm_sum[None, :]
    dpre16 = (dfeat * 2.0 * act).astype(jnp.bfloat16)
    enc_term = lax.dot_general(
        xg, dpre16, (((0,), (0,)), ((), ())), preferred_element_type=jnp.float32
    )
    enc_term = enc_term.reshape(2, half, local_latents)
    dec_term = 2.0 * lax.dot_general(
        feats16, err16, (((0,), (0,)), ((), ())), preferred_element_type=jnp.float32
    )
    scale = jnp.where(
        column_ids[None, :] < half, (feat_sum / norm_base)[:, None], (feat_sum / norm_inst)[:, None]
    )
    dec_term = dec_term + sparsity_weight * scale * w_dec.astype(jnp.float32)
    enc_total = lax.psum_scatter(
        enc_term.astype(jnp.bfloat16), "dp", scatter_dimension=1, tiled=True
    ).astype(jnp.float32)
    dec_total = lax.psum_scatter(
        dec_term.astype(jnp.bfloat16), "dp", scatter_dimension=1, tiled=True
    ).astype(jnp.float32)
    total, count = lax.psum((local_loss, own_count), ("dp", "latent"))
    factor = loss_scale / count
    grad_enc = (enc_total * factor).astype(jnp.bfloat16)
    grad_dec = (dec_total * factor).astype(jnp.bfloat16)
    loss = total / (count * width)
    return (grad_enc, grad_dec, loss)


def solution(mesh):
    return jax.shard_map(
        shards,
        mesh=mesh,
        in_specs=(
            P(("dp", "latent"), None),
            P(("dp", "latent")),
            P(("dp", "latent"), None),
            P(None, None, "latent"),
            P("latent"),
            P("latent", None),
            P(),
        ),
        out_specs=(P(None, "dp", "latent"), P("latent", "dp"), P()),
        check_vma=False,
    )
```

profile of v0, /device:TPU:1, one launch (start us, length us, event | category | flops | bytes accessed | tf_op | source)
XLA Modules:
  0.0 414.3 jit_solution(3964806186658669848)
XLA Ops:
  7.2 1.6 sort.17
  8.9 0.6 gather_fusion
  9.5 0.5 broadcast.57
  10.0 0.7 reduce.2
  10.7 0.1 reshape.95
  10.8 10.1 %all_to_all.14 = bf16[4,2,4096]{2,1,0:T(2,128)(2,1)S(1)} all-to-all(bf16[4,2,4096]{2,1,0:T(2,128)(2,1)S(1)} %reshape.95), channel_id=1, replica_groups=mesh['dp'=4,'latent'=32] {'dp'}, dimensions={0} | all-to-all | bytes 131072 | tf_op jit(solution)/shard_map/all_to_all | solution.py:25
  20.9 0.7 reshape.96
  22.3 0.6 gather_fusion.1
  23.0 0.6 fusion.25
  23.6 0.7 copy.17
  24.3 3.2 all-to-all-start.1
  27.5 1.3 dynamic-slice
  29.6 1.9 all-to-all-done.1
  31.5 0.1 reduce.1
  31.6 0.2 dynamic-update-slice
  31.8 65.9 %all-reduce = bf16[128]{0:T(256)(128)(2,1)S(1)} all-reduce(bf16[128]{0:T(256)(128)(2,1)S(1)} %dynamic-update-slice), channel_id=2, replica_groups=mesh['dp'=4,'latent'=32] {'latent'}, use_global_device_ids=true, to_apply=%add | all-reduce | flops 128 | bytes 512
  97.8 7.3 %multiply_reduce_fusion = (f32[512]{0:T(512)S(1)}, f32[128,512]{1,0:T(8,128)S(1)}) fusion(f32[128]{0:T(128)S(1)} %mul.102, f32[512]{0:T(512)} %param.11, bf16[8192,512]{1,0:T(8,128)(2,1)} %bitcast.33, bf16[128,1,8192]{2,1,0:T(2,128)(2,1)} %all-gather.3.cloned.1.call-done), kind=kOutput, calls=%fused_computation.26 | convolution fusion | flops 1074068992 | bytes 10752512 | tf_op jit(solution)/shard_map/dot_general | solution.py:44
  105.1 6.0 %convolution_convert_fusion = bf16[128,8192]{1,0:T(8,128)(2,1)} fusion(bf16[512,8192]{1,0:T(8,128)(2,1)} %param.12, f32[128,512]{1,0:T(8,128)S(1)} %get-tuple-element.16), kind=kOutput, calls=%fused_computation.6 | convolution fusion | flops 1074921472 | bytes 10747904 | tf_op jit(solution)/shard_map/dot_general | solution.py:48
  111.1 0.2 reduce-scatter.3.cloned.1.call-start
  111.3 11.3 %convert_multiply_fusion.1 = f32[512,8192]{1,0:T(8,128)} fusion(bf16[512,8192]{1,0:T(8,128)(2,1)} %param.12), kind=kLoop, calls=%fused_computation.3 | loop fusion | flops 8388608 | bytes 25165824 | tf_op jit(solution)/shard_map/square | solution.py:38
  122.6 6.5 %slice_reduce_fusion.1 = (f32[512]{0:T(512)S(1)}, f32[512]{0:T(512)S(1)}) fusion(f32[512,8192]{1,0:T(8,128)} %convert_multiply_fusion.1), kind=kLoop, calls=%fused_computation.8 | loop fusion | flops 4193280 | bytes 16781312 | tf_op jit(solution)/shard_map/reduce_sum | solution.py:39
  129.2 8.8 %copy.19 = bf16[128,1,8192]{0,2,1:T(8,128)(2,1)S(1)} copy(bf16[128,1,8192]{2,1,0:T(2,128)(2,1)} %all-gather.3.cloned.1.call-done) | data formatting | bytes 4194304 | tf_op jit(solution)/shard_map/dot_general | solution.py:61
  138.0 0.6 multiply_reduce_fusion.2
  138.6 75.9 %all-reduce.4.cloned.1.call-done = bf16[128,8192]{1,0:T(8,128)(2,1)} async-done(((bf16[128,8192]{1,0:T(8,128)(2,1)}), bf16[128,8192]{1,0:T(8,128)(2,1)}) %all-reduce.4.cloned.1.call-update) | async-done | bytes 2097168 | tf_op jit(solution)/shard_map/psum | solution.py:49
  214.5 8.7 %subtract_multiply_fusion = f32[128,8192]{1,0:T(8,128)} fusion(bf16[128,8192]{1,0:T(8,128)(2,1)} %all-reduce.4.cloned.1.call-done, f32[128]{0:T(128)S(1)} %mul.102, f32[8192]{0:T(1024)S(1)} %bitcast.36, bf16[128,1,8192]{2,1,0:T(2,128)(2,1)} %all-gather.3.cloned.1.call-done), kind=kLoop, calls=%fused_computation.12 | loop fusion | flops 5242880 | bytes 8421888 | tf_op jit(solution)/shard_map/mul | solution.py:50
  223.2 15.0 %convolution_convert_fusion.1 = bf16[2,4096,512]{2,1,0:T(8,128)(2,1)} fusion(bf16[2,4096,128]{2,1,0:T(8,128)(2,1)S(1)} %bitcast.34, f32[128,512]{1,0:T(8,128)S(1)} %get-tuple-element.16, bf16[512,8192]{1,0:T(8,128)(2,1)} %param.12, f32[128,8192]{1,0:T(8,128)} %subtract_multiply_fusion, f32[512]{0:T(512)S(1)} %get-tuple-element.10, f32[128]{0:T(128)S(1)} %mul.102), kind=kOutput, calls=%fused_computation.9 | convolution fusion | flops 2153119744 | bytes 23333376 | tf_op jit(solution)/shard_map/dot_general | solution.py:61
  238.3 9.8 %fusion.1 = bf16[512,8192]{1,0:T(8,128)(2,1)} fusion(bf16[512,8192]{1,0:T(8,128)(2,1)} %param.12, f32[512]{0:T(512)S(1)} %get-tuple-element.12, f32[512]{0:T(512)S(1)} %get-tuple-element.11, pred[8192]{0:T(1024)(128)(4,1)S(1)} %iota_compare_fusion, f32[128,8192]{1,0:T(8,128)} %subtract_multiply_fusion, f32[128,512]{1,0:T(8,128)S(1)} %get-tuple-element.16), kind=kOutput, calls=%fused_computation.5 | convolution fusion | flops 1100087296 | bytes 21245952 | tf_op jit(solution)/shard_map/dot_general | solution.py:65
  248.1 1.6 multiply_reduce_fusion.1
  251.0 69.5 %all-reduce.1 = (f32[]{:T(128)}, f32[]{:T(128)}) all-reduce(f32[]{:T(128)} %get-tuple-element.13, f32[]{:T(128)S(6)} %add.86), channel_id=1, replica_groups=mesh['dp'=4,'latent'=32] {'dp','latent'}, use_global_device_ids=true, to_apply=%region_6.7 | all-reduce | flops 2 | bytes 16 | tf_op jit(solution)/shard_map/psum | solution.py:78
  322.5 3.3 multiply_convert_fusion.1
  325.8 77.3 %reduce-scatter.5.cloned.1.call-done = bf16[512,2048]{1,0:T(8,128)(2,1)} async-done(((bf16[512,8192]{1,0:T(8,128)(2,1)}), bf16[512,2048]{1,0:T(8,128)(2,1)}) %reduce-scatter.5.cloned.1.call-update) | async-done | bytes 2097168 | tf_op jit(solution)/shard_map/reduce_scatter | solution.py:75
  403.2 3.4 multiply_convert_fusion
  (23 shorter events, 0.3 us)
Async XLA Ops:
  7.2 1.7 copy-start
  7.2 90.6 %all-gather.3.cloned.1.call-start = ((), (), s32[]{:S(2)}) async-start(), calls=%async_computation.4 | async-start | bytes 4325376 | tf_op jit(solution)/shard_map/all_gather | solution.py:29
  24.3 7.2 %all-to-all-start.1 = ((bf16[4,1,1]{2,1,0:T(2,128)(2,1)}), bf16[4,1,1]{2,1,0:T(2,128)(2,1)S(1)}, u32[]{:S(2)}, u32[]{:S(2)}) async-start(bf16[4,1,1]{2,1,0:T(2,128)(2,1)} %copy.17), calls=%async_computation.1 | async-start | bytes 4096 | tf_op jit(solution)/shard_map/all_to_all | solution.py:26
  27.5 187.0 %all-reduce.4.cloned.1.call-start = ((), (), s32[]{:S(2)}) async-start(), calls=%async_computation.5 | async-start | bytes 4194304 | tf_op jit(solution)/shard_map/psum | solution.py:49
  111.1 11.6 %copy-start.2 = (f32[2,4096]{1,0:T(2,128)S(1)}, f32[2,4096]{1,0:T(2,128)}, u32[]{:S(2)}) copy-start(f32[2,4096]{1,0:T(2,128)} %param.13) | copy-start | bytes 98308
  111.1 211.4 %reduce-scatter.3.cloned.1.call-start = ((), (), s32[]{:S(2)}) async-start(), calls=%async_computation.6 | async-start | bytes 10485760 | tf_op jit(solution)/shard_map/reduce_scatter | solution.py:72
  238.2 165.0 %reduce-scatter.5.cloned.1.call-start = ((), (), s32[]{:S(2)}) async-start(), calls=%async_computation.7 | async-start | bytes 10485760 | tf_op jit(solution)/shard_map/reduce_scatter | solution.py:75
  321.8 84.8 %copy-start.1 = (bf16[5,8192]{1,0:T(8,128)(2,1)S(1)}, bf16[5,8192]{1,0:T(8,128)(2,1)}, u32[]{:S(2)}) copy-start(bf16[5,8192]{1,0:T(8,128)(2,1)} %param.7) | copy-start | bytes 245764
Sparse Core Ops, SparseCore 0:
  21.8 47.3 all-gather.2
  111.2 103.2 all-reduce.3
  238.3 82.5 reduce-scatter.2
  323.2 79.8 reduce-scatter.4
where the time goes:
time: 415 us; the launch traced here: 414 us
  waiting for transfers between devices  155 us (37%)
  blocking collectives  145 us (35%)
  other arithmetic  38.6 us (9%)
  matrix products  38 us (9%)
  between operations  19.7 us (5%)
  local copies, waits for them, and re-layouts  13.6 us (3%)
    reduce_scatter x1, waiting for transfers between devices, shards(): lax.psum_scatter(dec_term.astype(jnp.bfloat16), 'dp', scatter_dimension=1...  77.3 us
    psum x1, waiting for transfers between devices, shards(): lax.psum(partial_value.astype(jnp.bfloat16), 'latent').astype(jnp.float32)  75.9 us
    psum x1, blocking collectives, shards(): total, count = lax.psum((local_loss, own_count), ('dp', 'latent'))  69.5 us
    unnamed x1, blocking collectives  65.9 us
    dot_general x1, matrix products, shards(): lax.dot_general(xg, dpre16, (((0,), (0,)), ((), ())), preferred_element_t...  15 us
    square x1, other arithmetic, shards(): squares_dec = jnp.square(w_dec.astype(jnp.float32))  11.3 us
    all_to_all x1, blocking collectives, shards(): lax.all_to_all(outgoing, 'dp', split_axis=0, concat_axis=0, tiled=True)  10.1 us
    dot_general x1, matrix products, shards(): lax.dot_general(feats16, err16, (((0,), (0,)), ((), ())), preferred_eleme...  9.77 us
  transfers between devices with their start and end apart: 5, of which 3 were waited for; matrix products, arithmetic and copies ran while one was open for 11% of the time, Pallas kernels for 0%

commit v1 on v0

--- a/solution.py
+++ b/solution.py
@@ -75,7 +75,7 @@
     dec_total = lax.psum_scatter(
         dec_term.astype(jnp.bfloat16), "dp", scatter_dimension=1, tiled=True
     ).astype(jnp.float32)
-    total, count = lax.psum((local_loss, own_count), ("dp", "latent"))
+    total, count = lax.psum(lax.psum((local_loss, own_count), "dp"), "latent")
     factor = loss_scale / count
     grad_enc = (enc_total * factor).astype(jnp.bfloat16)
     grad_dec = (dec_total * factor).astype(jnp.bfloat16)

time: 415 us -> 414 us (level)
  waiting for transfers between devices: 155 us -> 148 us
  blocking collectives: 145 us -> 151 us
    reduce_scatter x1, waiting for transfers between devices: 77.3 us -> 70.3 us  [shards(): lax.psum_scatter(dec_term.astype(jnp.bfloat16), 'dp', scatter_dimension=1...]
    psum x1 -> x2, blocking collectives: 69.5 us -> 75.1 us  [shards(): total, count = lax.psum(lax.psum((local_loss, own_count), 'dp'), 'latent')]
where the time goes in v1:
time: 414 us; the launch traced here: 413 us
  blocking collectives  151 us (36%)
  waiting for transfers between devices  148 us (36%)
  other arithmetic  38.6 us (9%)
  matrix products  38 us (9%)
  between operations  19.7 us (5%)
  local copies, waits for them, and re-layouts  13.6 us (3%)
    psum x1, waiting for transfers between devices, shards(): lax.psum(partial_value.astype(jnp.bfloat16), 'latent').astype(jnp.float32)  75.9 us
    psum x2, blocking collectives, shards(): total, count = lax.psum(lax.psum((local_loss, own_count), 'dp'), 'latent')  75.1 us
    reduce_scatter x1, waiting for transfers between devices, shards(): lax.psum_scatter(dec_term.astype(jnp.bfloat16), 'dp', scatter_dimension=1...  70.3 us
    unnamed x1, blocking collectives  65.9 us
    dot_general x1, matrix products, shards(): lax.dot_general(xg, dpre16, (((0,), (0,)), ((), ())), preferred_element_t...  15 us
    square x1, other arithmetic, shards(): squares_dec = jnp.square(w_dec.astype(jnp.float32))  11.3 us
    all_to_all x1, blocking collectives, shards(): lax.all_to_all(outgoing, 'dp', split_axis=0, concat_axis=0, tiled=True)  10.1 us
    dot_general x1, matrix products, shards(): lax.dot_general(feats16, err16, (((0,), (0,)), ((), ())), preferred_eleme...  9.77 us
  transfers between devices with their start and end apart: 5, of which 3 were waited for; matrix products, arithmetic and copies ran while one was open for 11% of the time, Pallas kernels for 0%

profile of v1, /device:TPU:1, one launch (start us, length us, event | category | flops | bytes accessed | tf_op | source)
XLA Modules:
  0.0 412.8 jit_solution(10491689202695144847)
XLA Ops:
  7.2 1.6 sort.17
  8.9 0.6 gather_fusion
  9.5 0.5 broadcast.57
  10.0 0.7 reduce.2
  10.8 10.1 %all_to_all.14 = bf16[4,2,4096]{2,1,0:T(2,128)(2,1)S(1)} all-to-all(bf16[4,2,4096]{2,1,0:T(2,128)(2,1)S(1)} %reshape.95), channel_id=1, replica_groups=mesh['dp'=4,'latent'=32] {'dp'}, dimensions={0} | all-to-all | bytes 131072 | tf_op jit(solution)/shard_map/all_to_all | solution.py:25
  20.9 0.7 reshape.96
  22.3 0.6 gather_fusion.1
  23.0 0.6 fusion.25
  23.6 0.7 copy.17
  24.3 3.2 all-to-all-start.1
  27.5 1.3 dynamic-slice
  29.6 1.9 all-to-all-done.1
  31.5 0.1 reduce.1
  31.6 0.2 dynamic-update-slice
  31.8 65.9 %all-reduce = bf16[128]{0:T(256)(128)(2,1)S(1)} all-reduce(bf16[128]{0:T(256)(128)(2,1)S(1)} %dynamic-update-slice), channel_id=2, replica_groups=mesh['dp'=4,'latent'=32] {'latent'}, use_global_device_ids=true, to_apply=%add | all-reduce | flops 128 | bytes 512
  97.8 7.3 %multiply_reduce_fusion = (f32[512]{0:T(512)S(1)}, f32[128,512]{1,0:T(8,128)S(1)}) fusion(f32[128]{0:T(128)S(1)} %mul.102, f32[512]{0:T(512)} %param.11, bf16[8192,512]{1,0:T(8,128)(2,1)} %bitcast.33, bf16[128,1,8192]{2,1,0:T(2,128)(2,1)} %all-gather.3.cloned.1.call-done), kind=kOutput, calls=%fused_computation.26 | convolution fusion | flops 1074068992 | bytes 10752512 | tf_op jit(solution)/shard_map/dot_general | solution.py:44
  105.1 6.0 %convolution_convert_fusion = bf16[128,8192]{1,0:T(8,128)(2,1)} fusion(bf16[512,8192]{1,0:T(8,128)(2,1)} %param.12, f32[128,512]{1,0:T(8,128)S(1)} %get-tuple-element.18), kind=kOutput, calls=%fused_computation.6 | convolution fusion | flops 1074921472 | bytes 10747904 | tf_op jit(solution)/shard_map/dot_general | solution.py:48
  111.1 0.2 reduce-scatter.3.cloned.1.call-start
  111.3 11.3 %convert_multiply_fusion.1 = f32[512,8192]{1,0:T(8,128)} fusion(bf16[512,8192]{1,0:T(8,128)(2,1)} %param.12), kind=kLoop, calls=%fused_computation.3 | loop fusion | flops 8388608 | bytes 25165824 | tf_op jit(solution)/shard_map/square | solution.py:38
  122.6 6.5 %slice_reduce_fusion.1 = (f32[512]{0:T(512)S(1)}, f32[512]{0:T(512)S(1)}) fusion(f32[512,8192]{1,0:T(8,128)} %convert_multiply_fusion.1), kind=kLoop, calls=%fused_computation.8 | loop fusion | flops 4193280 | bytes 16781312 | tf_op jit(solution)/shard_map/reduce_sum | solution.py:39
  129.2 8.8 %copy.19 = bf16[128,1,8192]{0,2,1:T(8,128)(2,1)S(1)} copy(bf16[128,1,8192]{2,1,0:T(2,128)(2,1)} %all-gather.3.cloned.1.call-done) | data formatting | bytes 4194304 | tf_op jit(solution)/shard_map/dot_general | solution.py:61
  138.0 0.6 multiply_reduce_fusion.2
  138.6 75.9 %all-reduce.5.cloned.1.call-done = bf16[128,8192]{1,0:T(8,128)(2,1)} async-done(((bf16[128,8192]{1,0:T(8,128)(2,1)}), bf16[128,8192]{1,0:T(8,128)(2,1)}) %all-reduce.5.cloned.1.call-update) | async-done | bytes 2097168 | tf_op jit(solution)/shard_map/psum | solution.py:49
  214.5 8.7 %subtract_multiply_fusion = f32[128,8192]{1,0:T(8,128)} fusion(bf16[128,8192]{1,0:T(8,128)(2,1)} %all-reduce.5.cloned.1.call-done, f32[128]{0:T(128)S(1)} %mul.102, f32[8192]{0:T(1024)S(1)} %bitcast.36, bf16[128,1,8192]{2,1,0:T(2,128)(2,1)} %all-gather.3.cloned.1.call-done), kind=kLoop, calls=%fused_computation.12 | loop fusion | flops 5242880 | bytes 8421888 | tf_op jit(solution)/shard_map/mul | solution.py:50
  223.2 15.0 %convolution_convert_fusion.1 = bf16[2,4096,512]{2,1,0:T(8,128)(2,1)} fusion(bf16[2,4096,128]{2,1,0:T(8,128)(2,1)S(1)} %bitcast.34, f32[128,512]{1,0:T(8,128)S(1)} %get-tuple-element.18, bf16[512,8192]{1,0:T(8,128)(2,1)} %param.12, f32[128,8192]{1,0:T(8,128)} %subtract_multiply_fusion, f32[512]{0:T(512)S(1)} %get-tuple-element.12, f32[128]{0:T(128)S(1)} %mul.102), kind=kOutput, calls=%fused_computation.9 | convolution fusion | flops 2153119744 | bytes 23333376 | tf_op jit(solution)/shard_map/dot_general | solution.py:61
  238.3 9.8 %fusion.1 = bf16[512,8192]{1,0:T(8,128)(2,1)} fusion(bf16[512,8192]{1,0:T(8,128)(2,1)} %param.12, f32[512]{0:T(512)S(1)} %get-tuple-element.14, f32[512]{0:T(512)S(1)} %get-tuple-element.13, pred[8192]{0:T(1024)(128)(4,1)S(1)} %iota_compare_fusion, f32[128,8192]{1,0:T(8,128)} %subtract_multiply_fusion, f32[128,512]{1,0:T(8,128)S(1)} %get-tuple-element.18), kind=kOutput, calls=%fused_computation.5 | convolution fusion | flops 1100087296 | bytes 21245952 | tf_op jit(solution)/shard_map/dot_general | solution.py:65
  248.1 1.6 multiply_reduce_fusion.1
  251.0 10.2 %all-reduce.2 = (f32[]{:T(128)}, f32[]{:T(128)}) all-reduce(f32[]{:T(128)} %get-tuple-element.15, f32[]{:T(128)S(6)} %add.90), channel_id=1, replica_groups=mesh['dp'=4,'latent'=32] {'dp'}, use_global_device_ids=true, to_apply=%region_6.7 | all-reduce | flops 2 | bytes 16 | tf_op jit(solution)/shard_map/psum | solution.py:78
  261.2 64.9 %all-reduce.1 = (f32[]{:T(128)}, f32[]{:T(128)}) all-reduce(f32[]{:T(128)} %get-tuple-element.9, f32[]{:T(128)} %get-tuple-element.10), channel_id=1, replica_groups=mesh['dp'=4,'latent'=32] {'latent'}, use_global_device_ids=true, to_apply=%region_7.8 | all-reduce | flops 2 | bytes 16 | tf_op jit(solution)/shard_map/psum | solution.py:78
  328.1 3.3 multiply_convert_fusion.1
  331.5 70.3 %reduce-scatter.5.cloned.1.call-done = bf16[512,2048]{1,0:T(8,128)(2,1)} async-done(((bf16[512,8192]{1,0:T(8,128)(2,1)}), bf16[512,2048]{1,0:T(8,128)(2,1)}) %reduce-scatter.5.cloned.1.call-update) | async-done | bytes 2097168 | tf_op jit(solution)/shard_map/reduce_scatter | solution.py:75
  401.7 3.4 multiply_convert_fusion
  (24 shorter events, 0.4 us)
Async XLA Ops:
  7.2 1.7 copy-start
  7.2 90.6 %all-gather.3.cloned.1.call-start = ((), (), s32[]{:S(2)}) async-start(), calls=%async_computation.4 | async-start | bytes 4325376 | tf_op jit(solution)/shard_map/all_gather | solution.py:29
  24.3 7.2 %all-to-all-start.1 = ((bf16[4,1,1]{2,1,0:T(2,128)(2,1)}), bf16[4,1,1]{2,1,0:T(2,128)(2,1)S(1)}, u32[]{:S(2)}, u32[]{:S(2)}) async-start(bf16[4,1,1]{2,1,0:T(2,128)(2,1)} %copy.17), calls=%async_computation.1 | async-start | bytes 4096 | tf_op jit(solution)/shard_map/all_to_all | solution.py:26
  27.5 187.0 %all-reduce.5.cloned.1.call-start = ((), (), s32[]{:S(2)}) async-start(), calls=%async_computation.5 | async-start | bytes 4194304 | tf_op jit(solution)/shard_map/psum | solution.py:49
  111.1 11.6 %copy-start.2 = (f32[2,4096]{1,0:T(2,128)S(1)}, f32[2,4096]{1,0:T(2,128)}, u32[]{:S(2)}) copy-start(f32[2,4096]{1,0:T(2,128)} %param.13) | copy-start | bytes 98308
  111.1 217.1 %reduce-scatter.3.cloned.1.call-start = ((), (), s32[]{:S(2)}) async-start(), calls=%async_computation.6 | async-start | bytes 10485760 | tf_op jit(solution)/shard_map/reduce_scatter | solution.py:72
  238.2 163.5 %reduce-scatter.5.cloned.1.call-start = ((), (), s32[]{:S(2)}) async-start(), calls=%async_computation.7 | async-start | bytes 10485760 | tf_op jit(solution)/shard_map/reduce_scatter | solution.py:75
  327.4 77.8 %copy-start.1 = (bf16[5,8192]{1,0:T(8,128)(2,1)S(1)}, bf16[5,8192]{1,0:T(8,128)(2,1)}, u32[]{:S(2)}) copy-start(bf16[5,8192]{1,0:T(8,128)(2,1)} %param.7) | copy-start | bytes 245764
Sparse Core Ops, SparseCore 0:
  21.8 47.3 all-gather.2
  111.2 103.2 all-reduce.4
  238.3 80.7 reduce-scatter.2
  321.5 80.2 reduce-scatter.4
